TPU v7x, 32 devices: a whole 2x2x4 slice. The times are simulated.
32 devices in a mesh: row: 8 (over z, x), col: 4 (over y, core).
Axes of the slice: x: 2, y: 2, z: 4, core: 2. Of those that a mesh axis runs over, the one named last changes fastest.
Arguments:
- charges: float32 [32768], P(('row', 'col')), may hold values from -0.5 to 1.5
- structure_id: int32 [32768], P(('row', 'col')), may hold values from 0 to 255, as said below
- live_count: int32 [32], P(('row', 'col')), may hold values from 512 to 1024, as said below
- cell_index: int32 [3, 32768], P(None, ('row', 'col')), may hold values from 0 to 255, as said below
- fraction: float32 [3, 32768], P(None, ('row', 'col')), may hold values from 0 to 1
- influence: float32 [256, 64, 64], P('col', 'row'), may hold values from 0.1 to 10
Outputs:
- forces: float32 [3, 32768], P(None, ('row', 'col'))
- atom_energy: float32 [32768], P(('row', 'col'))
Inputs may be any that keep to these rules, and one draw needn't show every extreme that they name: `structure_id`: devices are numbered row-major over (row, col). Slots 0 to 7 of device d are live and belong to fragments d * 8 to d * 8 + 7, so every fragment has a live atom; every other slot names a fragment of its own device, of one of the four devices beside it along row or col (wrapping around), or of the device whose number is d plus half the number of devices (wrapping around). Device d's live atoms are its first live_count[d] slots; the count reaches 1024 on some device in every draw. `cell_index`: the atom slots of the device at (row r, col c) lie in its mesh block: first index from r * 8 to r * 8 + 7, second from c * 16 to c * 16 + 15; the third is anywhere.
All inputs are finite; a program needn't handle non-finite values.
Results may differ from a plain program's by a relative error of at most 0.000065.
Values sent between devices are 32-bit elements; how exact they have to be, the bound alone decides.
A program may use at most 64 MiB of HBM per device.

v0:
```python
import math

import jax
import jax.numpy as jnp
from jax import lax
from jax.sharding import PartitionSpec as P

CX = 8
CY = 16
NZ = 256
S_DEV = 8


highest = lax.Precision.HIGHEST


def passed_along(block, axis, distance):
    devices = range(lax.axis_size(axis))
    route = [((i - distance) % len(devices), i) for i in devices]
    return lax.ppermute(block, axis, route)


def spline_weights(fraction):
    remain = 1.0 - fraction
    square = fraction * fraction
    cubic_term = square * fraction
    values = [
        remain * remain * remain / 6.0,
        (3.0 * cubic_term - 6.0 * square + 4.0) / 6.0,
        (-3.0 * cubic_term + 3.0 * square + 3.0 * fraction + 1.0) / 6.0,
        cubic_term / 6.0,
    ]
    slopes = [
        -0.5 * remain * remain,
        0.5 * (3.0 * square - 4.0 * fraction),
        0.5 * (-3.0 * square + 2.0 * fraction + 1.0),
        0.5 * square,
    ]
    return (values, slopes)


def place_weights(weights, local, width, period):
    columns = lax.broadcasted_iota(jnp.int32, (local.shape[0], width), 1)
    result = jnp.zeros((local.shape[0], width), jnp.float32)
    for offset in range(4):
        target = (local + offset) % period
        result = result + jnp.where(columns == target[:, None], weights[offset][:, None], 0.0)
    return result


def dft_tables(length):
    counter = lax.iota(jnp.int32, length)
    product = counter[:, None] * counter[None, :] % length
    angle = 2.0 * math.pi / length * product.astype(jnp.float32)
    return (jnp.cos(angle), jnp.sin(angle))


def rotate_pair(real_part, imag_part, pattern, cosine, sine, direction):
    real_cos = jnp.einsum(pattern, real_part, cosine, precision=highest)
    real_sin = jnp.einsum(pattern, real_part, sine, precision=highest)
    imag_cos = jnp.einsum(pattern, imag_part, cosine, precision=highest)
    imag_sin = jnp.einsum(pattern, imag_part, sine, precision=highest)
    return (real_cos - direction * imag_sin, imag_cos + direction * real_sin)


def body(charges, structure_id, live_count, cell_index, fraction, influence):
    atom_total = charges.shape[0]
    row_count = lax.axis_size("row")
    col_count = lax.axis_size("col")
    mesh_x = CX * row_count
    mesh_y = CY * col_count
    structures = S_DEV * row_count * col_count
    local_x = cell_index[0] - lax.axis_index("row") * CX
    local_y = cell_index[1] - lax.axis_index("col") * CY
    live = (lax.iota(jnp.int32, atom_total) < live_count[0]).astype(jnp.float32)
    wx_val, wx_slope = spline_weights(fraction[0])
    wy_val, wy_slope = spline_weights(fraction[1])
    wz_val, wz_slope = spline_weights(fraction[2])
    big_period = 4 * (CX + CY + 8)
    x_rows = place_weights(wx_val, local_x, CX + 3, big_period)
    x_slope_rows = place_weights(wx_slope, local_x, CX + 3, big_period)
    y_rows = place_weights(wy_val, local_y, CY + 3, big_period)
    y_slope_rows = place_weights(wy_slope, local_y, CY + 3, big_period)
    z_rows = place_weights(wz_val, cell_index[2], NZ, NZ)
    z_slope_rows = place_weights(wz_slope, cell_index[2], NZ, NZ)
    plane = (y_rows[:, :, None] * x_rows[:, None, :]).reshape(atom_total, -1)
    charge_sums = jax.ops.segment_sum(charges * live, structure_id, num_segments=structures)
    live_sums = jax.ops.segment_sum(live, structure_id, num_segments=structures)
    totals, counts = lax.psum((charge_sums, live_sums), ("row", "col"))
    neutral = (charges - jnp.take(totals / counts, structure_id)) * live
    spread_grid = lax.dot_general(
        plane,
        neutral[:, None] * z_rows,
        (((0,), (0,)), ((), ())),
        precision=highest,
        preferred_element_type=jnp.float32,
    )
    extended = spread_grid.reshape(CY + 3, CX + 3, NZ)
    spill_x = passed_along(extended[:, CX:, :], "row", 1)
    extended = extended[:, :CX, :].at[:, :3, :].add(spill_x)
    spill_y = passed_along(extended[CY:], "col", 1)
    density = extended[:CY].at[:3].add(spill_y)
    cos_z, sin_z = dft_tables(NZ)
    cos_y, sin_y = dft_tables(mesh_y)
    cos_x, sin_x = dft_tables(mesh_x)
    real_z = jnp.einsum("yxz,zk->kxy", density, cos_z, precision=highest)
    imag_z = -jnp.einsum("yxz,zk->kxy", density, sin_z, precision=highest)
    columns = lax.all_to_all(
        jnp.stack([real_z, imag_z]), "col", split_axis=1, concat_axis=3, tiled=True
    )
    real_y, imag_y = rotate_pair(columns[0], columns[1], "zxy,yk->zkx", cos_y, sin_y, -1.0)
    rows = lax.all_to_all(
        jnp.stack([real_y, imag_y]), "row", split_axis=2, concat_axis=3, tiled=True
    )
    real_x, imag_x = rotate_pair(rows[0], rows[1], "zyx,xk->zyk", cos_x, sin_x, -1.0)
    scale = influence / float(mesh_x * mesh_y * NZ)
    real_x = real_x * scale
    imag_x = imag_x * scale
    back_x, back_x_imag = rotate_pair(real_x, imag_x, "zyk,kx->zyx", cos_x, sin_x, 1.0)
    returned = lax.all_to_all(
        jnp.stack([back_x, back_x_imag]), "row", split_axis=3, concat_axis=2, tiled=True
    )
    back_y, back_y_imag = rotate_pair(returned[0], returned[1], "zkx,ky->zxy", cos_y, sin_y, 1.0)
    whole_z = lax.all_to_all(
        jnp.stack([back_y, back_y_imag]), "col", split_axis=3, concat_axis=1, tiled=True
    )
    potential = jnp.einsum("kxy,kz->yxz", whole_z[0], cos_z, precision=highest) - jnp.einsum(
        "kxy,kz->yxz", whole_z[1], sin_z, precision=highest
    )
    upper_x = passed_along(potential[:, :3, :], "row", -1)
    widened = jnp.concatenate([potential, upper_x], axis=1)
    upper_y = passed_along(widened[:3], "col", -1)
    widened = jnp.concatenate([widened, upper_y], axis=0).reshape(-1, NZ)
    sampled = lax.dot_general(
        jnp.concatenate([z_rows, z_slope_rows], axis=0),
        widened,
        (((1,), (1,)), ((), ())),
        precision=highest,
        preferred_element_type=jnp.float32,
    )
    sample_val = sampled[:atom_total]
    sample_slope = sampled[atom_total:]
    plane_dx = (y_rows[:, :, None] * x_slope_rows[:, None, :]).reshape(atom_total, -1)
    plane_dy = (y_slope_rows[:, :, None] * x_rows[:, None, :]).reshape(atom_total, -1)
    value = jnp.sum(plane * sample_val, axis=1)
    grad_x = jnp.sum(plane_dx * sample_val, axis=1)
    grad_y = jnp.sum(plane_dy * sample_val, axis=1)
    grad_z = jnp.sum(plane * sample_slope, axis=1)
    atom_energy = 0.5 * neutral * value
    forces = -neutral[None, :] * jnp.stack([grad_x, grad_y, grad_z])
    return (forces, atom_energy)


def solution(mesh):
    placed = (
        P(("row", "col")),
        P(("row", "col")),
        P(("row", "col")),
        P(None, ("row", "col")),
        P(None, ("row", "col")),
        P("col", "row", None),
    )
    return jax.shard_map(
        body,
        mesh=mesh,
        in_specs=placed,
        out_specs=(P(None, ("row", "col")), P(("row", "col"))),
        check_vma=False,
    )
```

profile of v0, /device:TPU:9, one launch (start us, length us, event | category | flops | bytes accessed | tf_op | source)
XLA Modules:
  0.0 170.3 jit_solution(16986416854421868476)
XLA Ops:
  2.7 7.7 %scatter_custom_fusion = f32[256]{0:T(256)S(1)} fusion(s32[1024]{0:T(1024)} %param.11, f32[1024]{0:T(1024)S(1)} %fusion.131, f32[]{:T(128)} %constant.237.clone.1), kind=kCustom, calls=%fused_computation.243 | custom fusion | flops 1024 | bytes 1536 | tf_op jit(solution)/shard_map/scatter-add | solution.py:87
  10.4 7.7 %scatter_custom_fusion.1 = f32[256]{0:T(256)S(1)} fusion(s32[1024]{0:T(1024)} %param.11, f32[1024]{0:T(1024)S(1)} %fusion.130, f32[]{:T(128)} %constant.237.clone.1), kind=kCustom, calls=%fused_computation.241 | custom fusion | flops 1024 | bytes 1536 | tf_op jit(solution)/shard_map/scatter-add | solution.py:88
  20.1 1.9 %broadcast_multiply_fusion.2 = (f32[1024,19,11]{0,2,1:T(8,128)}, f32[1024,19,11]{0,2,1:T(8,128)S(1)}, f32[1024,19,11]{0,2,1:T(8,128)}) fusion(f32[1024,11]{0,1:T(8,128)S(1)} %get-tuple-element.45, f32[1024,19]{0,1:T(8,128)S(1)} %get-tuple-element.48, f32[1024,11]{0,1:T(8,128)S(1)} %get-tuple-element.46, f32[1024,19]{0,1:T(8,128)S(1)} %get-tuple-element.47), kind=kLoop, calls=%fused_computation.46 | loop fusion | flops 642048 | bytes 2813952 | tf_op jit(solution)/shard_map/mul | solution.py:143
  22.3 39.6 %all-reduce = (f32[256]{0:T(256)S(1)}, f32[256]{0:T(256)S(1)}) all-reduce(f32[256]{0:T(256)S(1)} %scatter_custom_fusion, f32[256]{0:T(256)S(1)} %scatter_custom_fusion.1), channel_id=1, replica_groups=mesh['row'=8,'col'=4] {'row','col'}, use_global_device_ids=true, to_apply=%region_1.2 | all-reduce | flops 512 | bytes 4096 | tf_op jit(solution)/shard_map/psum | solution.py:89
  62.0 6.8 %gather_fusion = f32[1024]{0:T(1024)S(1)} fusion(f32[256]{0:T(256)S(1)} %div.45, s32[1024]{0:T(1024)S(1)} %fusion.132), kind=kCustom, calls=%fused_computation | custom fusion | bytes 12288 | tf_op jit(solution)/shard_map/jit(_take)/gather | solution.py:90
  69.5 2.2 %fusion.17 = f32[19,11,256]{2,1,0:T(8,128)S(1)} fusion(f32[19,11,1024]{2,1,0:T(8,128)S(1)} %dot_general.71, f32[1024]{0:T(1024)S(1)} %get-tuple-element.94, f32[1024]{0:T(1024)S(1)} %get-tuple-element.79, s32[1024]{0:T(1024)S(1)} %get-tuple-element.84, f32[1024]{0:T(1024)S(1)} %get-tuple-element.78, s32[1024]{0:T(1024)S(1)} %get-tuple-element.83, ...), kind=kOutput, calls=%fused_computation.30 | convolution fusion | flops 660602880 | bytes 1106944 | tf_op jit(solution)/shard_map/dot_general | solution.py:91
  72.9 3.1 %collective-permute-done = f32[19,3,256]{2,1,0:T(4,128)S(1)} collective-permute-done((f32[19,3,256]{2,1,0:T(4,128)S(1)}, f32[19,3,256]{2,1,0:T(4,128)S(1)}, u32[]{:S(2)}, u32[]{:S(2)}) %collective-permute-start) | collective-permute-done | bytes 58400 | tf_op jit(solution)/shard_map/ppermute | solution.py:20
  76.3 4.6 %collective-permute-start.1 = (f32[3,8,256]{2,1,0:T(8,128)S(1)}, f32[3,8,256]{2,1,0:T(8,128)S(1)}, u32[]{:S(2)}, u32[]{:S(2)}) collective-permute-start(f32[3,8,256]{2,1,0:T(8,128)S(1)} %slice.156), channel_id=1, source_target_pairs={{3,0},{0,1},{1,2},{2,3},{7,4},{4,5},{5,6},{6,7},{11,8},{8,9},{9,10... | collective-permute-start | bytes 73736 | tf_op jit(solution)/shard_map/ppermute | solution.py:20
  81.8 1.3 fusion.16
  83.1 1.3 convolution_bitcast_fusion
  84.4 1.3 copy.81
  86.5 8.7 %all_to_all.60 = f32[4,1,16384]{2,1,0:T(1,128)S(1)} all-to-all(f32[4,1,16384]{2,1,0:T(1,128)S(1)} %reshape.1016), channel_id=1, replica_groups=mesh['row'=8,'col'=4] {'col'}, dimensions={0} | all-to-all | bytes 524288 | tf_op jit(solution)/shard_map/all_to_all | solution.py:108
  95.8 1.3 reduce.4
  101.9 10.7 %all_to_all.61 = f32[8,1,8192]{2,1,0:T(1,128)S(1)} all-to-all(f32[8,1,8192]{2,1,0:T(1,128)S(1)} %reshape.1018), channel_id=1, replica_groups=mesh['row'=8,'col'=4] {'row'}, dimensions={0} | all-to-all | bytes 524288 | tf_op jit(solution)/shard_map/all_to_all | solution.py:112
  119.4 11.4 %all_to_all.62 = f32[8,1,8192]{2,1,0:T(1,128)S(1)} all-to-all(f32[8,1,8192]{2,1,0:T(1,128)S(1)} %reshape.1020), channel_id=1, replica_groups=mesh['row'=8,'col'=4] {'row'}, dimensions={0} | all-to-all | bytes 524288 | tf_op jit(solution)/shard_map/all_to_all | solution.py:120
  135.6 10.9 %all_to_all.63 = f32[4,1,16384]{2,1,0:T(1,128)S(1)} all-to-all(f32[4,1,16384]{2,1,0:T(1,128)S(1)} %reshape.1022), channel_id=1, replica_groups=mesh['row'=8,'col'=4] {'col'}, dimensions={0} | all-to-all | bytes 524288 | tf_op jit(solution)/shard_map/all_to_all | solution.py:124
  146.4 1.3 reduce.7
  148.6 1.3 fusion.45
  150.3 1.3 fusion.42
  151.7 1.6 collective-permute-start.2
  153.3 1.4 collective-permute-done.2
  155.3 2.2 %collective-permute-start.3 = (f32[3,11,256]{2,0,1:T(4,128)}, f32[3,11,256]{2,0,1:T(4,128)}, u32[]{:S(2)}, u32[]{:S(2)}) collective-permute-start(f32[3,11,256]{2,0,1:T(4,128)} %pad_maximum_fusion.5), channel_id=1, source_target_pairs={{1,0},{2,1},{3,2},{0,3},{5,4},{6,5},{7,6},{4,7},{9,8},{10,9},{11,1... | collective-permute-start | bytes 101384 | tf_op jit(solution)/shard_map/ppermute | solution.py:20
  157.6 3.1 %select_add_fusion.1 = (f32[1024,256]{1,0:T(8,128)}, f32[1024,256]{1,0:T(8,128)}) fusion(f32[1024]{0:T(1024)S(1)} %copy-done.16, s32[1024]{0:T(1024)S(1)} %copy-done.26, f32[1024]{0:T(1024)S(1)} %copy-done.14, s32[1024]{0:T(1024)S(1)} %copy-done.24, f32[1024]{0:T(1024)S(1)} %copy-done.18, s32[1024]{0:T(1024)S(1)} %copy-done.22, f32[1024]{0:T(1024)S(1)} %copy-done.11, ...), kind=kLoop, calls=%fused_computation.34 | loop fusion | flops 4718592 | bytes 2146304 | tf_op jit(solution)/shard_map/add | solution.py:47
  165.1 3.3 %fusion = f32[2048,209]{0,1:T(8,128)S(1)} fusion(f32[209,256]{1,0:T(8,128)} %reshape.969, f32[1024,256]{1,0:T(8,128)S(1)} %copy-done.3, f32[1024,256]{1,0:T(8,128)S(1)} %copy-done.2), kind=kOutput, calls=%fused_computation.3 | convolution fusion | flops 1315438592 | bytes 4023296 | tf_op jit(solution)/shard_map/dot_general | solution.py:134
  (153 shorter events, 31.9 us)
Async XLA Ops:
  19.1 50.4 %copy-start.19 = (s32[1024]{0:T(1024)}, s32[1024]{0:T(1024)S(1)}, u32[]{:S(2)}) copy-start(s32[1024]{0:T(1024)S(1)} %get-tuple-element.81) | copy-start | bytes 12292
  19.1 50.4 %copy-start.21 = (s32[1024]{0:T(1024)}, s32[1024]{0:T(1024)S(1)}, u32[]{:S(2)}) copy-start(s32[1024]{0:T(1024)S(1)} %get-tuple-element.82) | copy-start | bytes 12292
  19.1 50.4 %copy-start.23 = (s32[1024]{0:T(1024)}, s32[1024]{0:T(1024)S(1)}, u32[]{:S(2)}) copy-start(s32[1024]{0:T(1024)S(1)} %get-tuple-element.83) | copy-start | bytes 12292
  19.1 50.4 %copy-start.25 = (s32[1024]{0:T(1024)}, s32[1024]{0:T(1024)S(1)}, u32[]{:S(2)}) copy-start(s32[1024]{0:T(1024)S(1)} %get-tuple-element.84) | copy-start | bytes 12292
  62.0 6.8 %copy-start.29 = (f32[1024]{0:T(1024)S(1)}, f32[1024]{0:T(1024)}, u32[]{:S(2)}) copy-start(f32[1024]{0:T(1024)} %param.10) | copy-start | bytes 12292
  62.0 6.9 %copy-start.30 = (s32[1024]{0:T(1024)S(1)}, s32[1024]{0:T(1024)}, u32[]{:S(2)}) copy-start(s32[1024]{0:T(1024)} %param.11) | copy-start | bytes 12292
  71.8 4.2 %collective-permute-start = (f32[19,3,256]{2,1,0:T(4,128)S(1)}, f32[19,3,256]{2,1,0:T(4,128)S(1)}, u32[]{:S(2)}, u32[]{:S(2)}) collective-permute-start(f32[19,3,256]{2,1,0:T(4,128)S(1)} %slice.153), channel_id=1, source_target_pairs={{28,0},{0,4},{4,8},{8,12},{12,16},{16,20},{20,24},{24,28},{29,1},{... | collective-permute-start | bytes 175112 | tf_op jit(solution)/shard_map/ppermute | solution.py:20
  76.3 5.5 %collective-permute-start.1 = (f32[3,8,256]{2,1,0:T(8,128)S(1)}, f32[3,8,256]{2,1,0:T(8,128)S(1)}, u32[]{:S(2)}, u32[]{:S(2)}) collective-permute-start(f32[3,8,256]{2,1,0:T(8,128)S(1)} %slice.156), channel_id=1, source_target_pairs={{3,0},{0,1},{1,2},{2,3},{7,4},{4,5},{5,6},{6,7},{11,8},{8,9},{9,10... | collective-permute-start | bytes 73736 | tf_op jit(solution)/shard_map/ppermute | solution.py:20
  149.9 7.6 %copy-start.7 = (f32[1024]{0:T(1024)S(1)}, f32[1024]{0:T(1024)}, u32[]{:S(2)}) copy-start(f32[1024]{0:T(1024)} %get-tuple-element.73) | copy-start | bytes 12292
  149.9 7.6 %copy-start.8 = (f32[1024]{0:T(1024)S(1)}, f32[1024]{0:T(1024)}, u32[]{:S(2)}) copy-start(f32[1024]{0:T(1024)} %get-tuple-element.74) | copy-start | bytes 12292
  149.9 7.6 %copy-start.9 = (f32[1024]{0:T(1024)S(1)}, f32[1024]{0:T(1024)}, u32[]{:S(2)}) copy-start(f32[1024]{0:T(1024)} %get-tuple-element.75) | copy-start | bytes 12292
  149.9 7.6 %copy-start.11 = (f32[1024]{0:T(1024)S(1)}, f32[1024]{0:T(1024)}, u32[]{:S(2)}) copy-start(f32[1024]{0:T(1024)} %copy-done.10) | copy-start | bytes 12292
  150.0 7.6 %copy-start.12 = (f32[1024]{0:T(1024)S(1)}, f32[1024]{0:T(1024)}, u32[]{:S(2)}) copy-start(f32[1024]{0:T(1024)} %get-tuple-element.77) | copy-start | bytes 12292
  150.0 7.6 %copy-start.14 = (f32[1024]{0:T(1024)S(1)}, f32[1024]{0:T(1024)}, u32[]{:S(2)}) copy-start(f32[1024]{0:T(1024)} %copy-done.13) | copy-start | bytes 12292
  150.0 7.6 %copy-start.16 = (f32[1024]{0:T(1024)S(1)}, f32[1024]{0:T(1024)}, u32[]{:S(2)}) copy-start(f32[1024]{0:T(1024)} %copy-done.15) | copy-start | bytes 12292
  150.0 7.6 %copy-start.18 = (f32[1024]{0:T(1024)S(1)}, f32[1024]{0:T(1024)}, u32[]{:S(2)}) copy-start(f32[1024]{0:T(1024)} %copy-done.17) | copy-start | bytes 12292
  150.0 7.6 %copy-start.20 = (s32[1024]{0:T(1024)S(1)}, s32[1024]{0:T(1024)}, u32[]{:S(2)}) copy-start(s32[1024]{0:T(1024)} %copy-done.19) | copy-start | bytes 12292
  150.0 7.6 %copy-start.22 = (s32[1024]{0:T(1024)S(1)}, s32[1024]{0:T(1024)}, u32[]{:S(2)}) copy-start(s32[1024]{0:T(1024)} %copy-done.21) | copy-start | bytes 12292
  150.0 7.6 %copy-start.24 = (s32[1024]{0:T(1024)S(1)}, s32[1024]{0:T(1024)}, u32[]{:S(2)}) copy-start(s32[1024]{0:T(1024)} %copy-done.23) | copy-start | bytes 12292
  150.0 7.6 %copy-start.26 = (s32[1024]{0:T(1024)S(1)}, s32[1024]{0:T(1024)}, u32[]{:S(2)}) copy-start(s32[1024]{0:T(1024)} %copy-done.25) | copy-start | bytes 12292
  151.7 9.0 %copy-start.1 = (f32[1024,19,11]{0,2,1:T(8,128)S(1)}, f32[1024,19,11]{0,2,1:T(8,128)}, u32[]{:S(2)}) copy-start(f32[1024,19,11]{0,2,1:T(8,128)} %get-tuple-element.42) | copy-start | bytes 2568196
  151.7 3.0 %collective-permute-start.2 = (f32[16,3,256]{2,0,1:T(8,128)S(1)}, f32[16,3,256]{2,0,1:T(8,128)S(1)}, u32[]{:S(2)}, u32[]{:S(2)}) collective-permute-start(f32[16,3,256]{2,0,1:T(8,128)S(1)} %slice.165), channel_id=1, source_target_pairs={{4,0},{8,4},{12,8},{16,12},{20,16},{24,20},{28,24},{0,28},{5,1},{9... | collective-permute-start | bytes 147464 | tf_op jit(solution)/shard_map/ppermute | solution.py:20
  155.3 8.1 %collective-permute-start.3 = (f32[3,11,256]{2,0,1:T(4,128)}, f32[3,11,256]{2,0,1:T(4,128)}, u32[]{:S(2)}, u32[]{:S(2)}) collective-permute-start(f32[3,11,256]{2,0,1:T(4,128)} %pad_maximum_fusion.5), channel_id=1, source_target_pairs={{1,0},{2,1},{3,2},{0,3},{5,4},{6,5},{7,6},{4,7},{9,8},{10,9},{11,1... | collective-permute-start | bytes 101384 | tf_op jit(solution)/shard_map/ppermute | solution.py:20
  165.1 3.3 %copy-start.5 = (f32[1024,209]{0,1:T(8,128)S(1)}, f32[1024,209]{0,1:T(8,128)}, u32[]{:S(2)}) copy-start(f32[1024,209]{0,1:T(8,128)} %mul.815) | copy-start | bytes 2568196
  (12 other events, 24.2 us)
where the time goes:
time: 172 us; the launch traced here: 170 us
  blocking collectives  81.4 us (47%)
  other arithmetic  32.2 us (19%)
  local copies, waits for them, and re-layouts  20.3 us (12%)
  matrix products  19.3 us (11%)
  starting transfers between devices  9.49 us (6%)
  waiting for transfers between devices  5.39 us (3%)
  between operations  2.24 us (1%)
    psum x1, blocking collectives, body(): totals, counts = lax.psum((charge_sums, live_sums), ('row', 'col'))  39.6 us
    all_to_all x1, blocking collectives, body(): lax.all_to_all(jnp.stack([back_x, back_x_imag]), 'row', split_axis=3, con...  11.4 us
    all_to_all x1, blocking collectives, body(): lax.all_to_all(jnp.stack([back_y, back_y_imag]), 'col', split_axis=3, con...  10.9 us
    all_to_all x1, blocking collectives, body(): lax.all_to_all(jnp.stack([real_y, imag_y]), 'row', split_axis=2, concat_a...  10.7 us
    ppermute x4, starting transfers between devices, passed_along(): return lax.ppermute(block, axis, route)  9.49 us
    all_to_all x1, blocking collectives, body(): lax.all_to_all(jnp.stack([real_z, imag_z]), 'col', split_axis=1, concat_a...  8.74 us
    scatter-add x1, other arithmetic, body(): live_sums = jax.ops.segment_sum(live, structure_id, num_segments=structures)  7.75 us
    scatter-add x1, other arithmetic, body(): jax.ops.segment_sum(charges * live, structure_id, num_segments=structures)  7.74 us
  transfers between devices with their start and end apart: 4, of which 3 were waited for; matrix products, arithmetic and copies ran while one was open for 3% of the time, Pallas kernels for 0%

commit v1 on v0

--- a/solution.py
+++ b/solution.py
@@ -1,8 +1,13 @@
 import math
+
+import functools
 
 import jax
 import jax.numpy as jnp
+import numpy as np
 from jax import lax
+from jax.experimental import pallas as pl
+from jax.experimental.pallas import tpu as pltpu
 from jax.sharding import PartitionSpec as P
 
 CX = 8
@@ -151,7 +156,433 @@
     return (forces, atom_energy)
 
 
+EXT_Y = CY + 3
+HALO_ROWS = 24
+PLANE = 256
+LANES = 128
+MESH = pl.DeviceIdType.MESH
+
+
+def plane_cells():
+    cells = np.zeros((PLANE, 2), np.int64)
+    used = np.zeros((PLANE,), bool)
+    for y in range(EXT_Y):
+        for x in range(CX):
+            cells[y * CX + x] = (x, y)
+            used[y * CX + x] = True
+    for x in range(3):
+        for y in range(EXT_Y):
+            cells[EXT_Y * CX + x * HALO_ROWS + y] = (CX + x, y)
+            used[EXT_Y * CX + x * HALO_ROWS + y] = True
+    return cells, used
+
+
+def make_plan(rows, cols):
+    n = rows * cols
+    offsets = [(0, 0), (1, 0), (-1, 0), (0, 1), (0, -1), (rows // 2, 0)]
+    distinct = len({(a % rows, b % cols) for a, b in offsets}) == len(offsets)
+    if not (
+        rows % 2 == 0
+        and cols % 2 == 0
+        and distinct
+        and NZ % (2 * n) == 0
+        and (NZ // n) % 8 == 0
+        and NZ % (cols * n) == 0
+        and (CY * cols) % rows == 0
+        and (CY * cols // rows) % cols == 0
+        and (NZ // n) * n == PLANE
+        and NZ // n // 2 * n == LANES
+    ):
+        return None
+    return (rows, cols, tuple(offsets))
+
+
+def make_tables(rows, cols):
+    n = rows * cols
+    half = NZ // n // 2
+    slots = 2 * half
+    z = np.arange(NZ)
+    forward_z = np.zeros((n, 2, half, NZ))
+    for p in range(n):
+        for j in range(half):
+            angle = 2 * np.pi * ((p + n * j) * z % NZ) / NZ
+            forward_z[p, 0, j] = np.cos(angle)
+            forward_z[p, 1, j] = -np.sin(angle)
+    forward_z[0, 1, 0] = 1.0 - 2.0 * (z % 2)
+    forward_z = forward_z.reshape(NZ, NZ)
+
+    r, c, m1, k1 = np.meshgrid(
+        np.arange(rows), np.arange(cols), np.arange(cols), np.arange(rows), indexing="ij"
+    )
+    phi = 2 * np.pi * ((k1 * r % rows) / rows + (m1 * c % cols) / cols)
+    phi = phi.reshape(n, n)
+    cosp, sinp = np.cos(phi), np.sin(phi)
+    gather = np.zeros((2, n, 2, half, 2, slots, n))
+    for kind in range(2):
+        for t in range(slots):
+            j, sign = t, 1.0
+            if t >= half:
+                j, sign = (slots - 1 - t if kind else slots - t), -1.0
+            if kind == 0 and t in (0, half):
+                part = 0 if t == 0 else 1
+                gather[kind, :, part, 0, 0, t] = cosp
+                gather[kind, :, part, 0, 1, t] = -sinp
+                continue
+            gather[kind, :, 0, j, 0, t] = cosp
+            gather[kind, :, 1, j, 0, t] = sign * sinp
+            gather[kind, :, 0, j, 1, t] = -sinp
+            gather[kind, :, 1, j, 1, t] = sign * cosp
+    gather = gather.reshape(2, n * 2 * half, 2 * slots * n)
+
+    cells, used = plane_cells()
+    x, y = cells[:, 0], cells[:, 1]
+    low_m, low_k = (v.reshape(-1) for v in np.meshgrid(np.arange(cols), np.arange(rows), indexing="ij"))
+    psi = 2 * np.pi * (
+        x[:, None] * low_k[None] / (CX * rows) + y[:, None] * low_m[None] / (CY * cols)
+    )
+    twiddle = np.stack([np.tile(np.cos(psi), (1, slots)), np.tile(np.sin(psi), (1, slots))])
+    high_m, high_k = (v.reshape(-1) for v in np.meshgrid(np.arange(CY), np.arange(CX), indexing="ij"))
+    chi = 2 * np.pi * (high_k[:, None] * x[None] % CX / CX + high_m[:, None] * y[None] % CY / CY)
+    cosc, sinc = np.cos(chi) * used[None], np.sin(chi) * used[None]
+    inner = np.block([[cosc, sinc], [-sinc, cosc]])
+    tables = (forward_z, gather, twiddle, inner, inner.T)
+    return tuple(np.ascontiguousarray(t).astype(np.float32) for t in tables)
+
+
+def dot(left, right, contract):
+    return lax.dot_general(
+        left,
+        right,
+        ((contract[:1], contract[1:]), ((), ())),
+        precision=highest,
+        preferred_element_type=jnp.float32,
+    )
+
+
+def pick(distance, weights):
+    result = jnp.where(distance == 3, weights[3], 0.0)
+    for i in (2, 1, 0):
+        result = jnp.where(distance == i, weights[i], result)
+    return result
+
+
+def kernel(
+    plan,
+    charges_ref, sid_ref, live_ref, cell_ref, frac_ref, influence_ref,
+    fz_hbm, gather_hbm, twiddle_hbm, inner_hbm, inner_t_hbm,
+    forces_ref, energy_ref,
+    fz, gather, twiddle, inner, inner_t,
+    z_rows, z_slopes, plane, x_rows, y_rows,
+    frag_out, frag_in, mean_out, mean_in,
+    kernel_in, field_out, field_in, back_out, back_in, sampled,
+    table_sems, frag_send, frag_recv, mean_send, mean_recv,
+    inf_send, inf_recv, field_send, field_recv, back_send, back_recv,
+):
+    rows, cols, offsets = plan
+    n = rows * cols
+    r, c = lax.axis_index("row"), lax.axis_index("col")
+    me = r * cols + c
+    atoms = charges_ref.shape[1]
+
+    def coords(p):
+        return (p // cols, lax.rem(p, cols))
+
+    barrier = pltpu.get_barrier_semaphore()
+
+    @pl.loop(1, n)
+    def _(o):
+        pl.semaphore_signal(
+            barrier, inc=1, device_id=coords(lax.rem(me + o, n)), device_id_type=MESH
+        )
+
+    tables = [
+        pltpu.make_async_copy(fz_hbm, fz, table_sems.at[0]),
+        pltpu.make_async_copy(gather_hbm.at[jnp.minimum(me, 1)], gather, table_sems.at[1]),
+        pltpu.make_async_copy(twiddle_hbm, twiddle, table_sems.at[2]),
+        pltpu.make_async_copy(inner_hbm, inner, table_sems.at[3]),
+        pltpu.make_async_copy(inner_t_hbm, inner_t, table_sems.at[4]),
+    ]
+    for table in tables:
+        table.start()
+
+    lane = lax.broadcasted_iota(jnp.int32, (1, atoms), 1)
+    live = (lane < live_ref[...]).astype(jnp.float32)
+    charges = charges_ref[...]
+    charged = charges * live
+    sid = sid_ref[...]
+    within = lax.broadcasted_iota(jnp.int32, (S_DEV, atoms), 0)
+    steps = [
+        (lax.rem(r + a % rows, rows), lax.rem(c + b % cols, cols)) for a, b in offsets
+    ]
+    senders = [
+        (lax.rem(r + (-a) % rows, rows), lax.rem(c + (-b) % cols, cols)) for a, b in offsets
+    ]
+
+    def belongs(o):
+        owner = steps[o][0] * cols + steps[o][1]
+        return sid == within + owner * S_DEV
+
+    def folded(values):
+        total = values[:, :LANES]
+        for k in range(1, atoms // LANES):
+            total = total + values[:, k * LANES : (k + 1) * LANES]
+        return total
+
+    for o in range(len(offsets)):
+        mine = belongs(o)
+        frag_out[o, :S_DEV] = folded(jnp.where(mine, charged, 0.0))
+        frag_out[o, S_DEV:] = folded(jnp.where(mine, live, 0.0))
+    pl.semaphore_wait(barrier, n - 1)
+    first = [
+        pltpu.make_async_remote_copy(
+            frag_out.at[o], frag_in.at[o], frag_send.at[o], frag_recv.at[o],
+            device_id=steps[o], device_id_type=MESH,
+        )
+        for o in range(1, len(offsets))
+    ]
+    for copy in first:
+        copy.start()
+
+    wx, vx = spline_weights(frac_ref[0:1, :])
+    wy, vy = spline_weights(frac_ref[1:2, :])
+    wz, vz = spline_weights(frac_ref[2:3, :])
+    cell_z = cell_ref[2:3, :]
+    step = 16
+
+    @pl.loop(0, NZ // step)
+    def _(b):
+        start = pl.multiple_of(b * step, step)
+        index = lax.broadcasted_iota(jnp.int32, (step, atoms), 0) + start - cell_z
+        distance = jnp.where(index < 0, index + NZ, index)
+        z_rows[pl.ds(start, step), :] = pick(distance, wz)
+        z_slopes[pl.ds(start, step), :] = pick(distance, vz)
+
+    distance = lax.broadcasted_iota(jnp.int32, (16, atoms), 0) - (cell_ref[0:1, :] - r * CX)
+    x_rows[0] = pick(distance, wx)
+    x_rows[1] = pick(distance, vx)
+    distance = lax.broadcasted_iota(jnp.int32, (HALO_ROWS, atoms), 0) - (
+        cell_ref[1:2, :] - c * CY
+    )
+    y_rows[0] = pick(distance, wy)
+    y_rows[1] = pick(distance, vy)
+
+    for copy in first:
+        copy.wait()
+    total = frag_out[0]
+    for o in range(1, len(offsets)):
+        total = total + frag_in[o]
+    charge_sum = jnp.sum(total[:S_DEV], axis=1, keepdims=True)
+    live_sum = jnp.sum(total[S_DEV:], axis=1, keepdims=True)
+    own_mean = charge_sum / live_sum
+    mean_out[...] = jnp.broadcast_to(own_mean, (S_DEV, LANES))
+    second = [
+        pltpu.make_async_remote_copy(
+            mean_out, mean_in.at[o], mean_send.at[o], mean_recv.at[o],
+            device_id=senders[o], device_id_type=MESH,
+        )
+        for o in range(1, len(offsets))
+    ]
+    for copy in second:
+        copy.start()
+
+    place = c * rows + r
+
+    def inf_copy(o):
+        p = lax.rem(me + o, n)
+        residue = jnp.where(c < cols // 2, p, lax.rem(n - p, n))
+        return pltpu.make_async_remote_copy(
+            influence_ref.at[residue], kernel_in.at[place], inf_send.at[o], inf_recv.at[o],
+            device_id=coords(p), device_id_type=MESH,
+        )
+
+    @pl.loop(1, n)
+    def _(o):
+        inf_copy(o).start()
+
+    own_inf = pltpu.make_async_copy(
+        influence_ref.at[jnp.where(c < cols // 2, me, lax.rem(n - me, n))],
+        kernel_in.at[place],
+        inf_recv.at[0],
+    )
+    own_inf.start()
+
+    for copy in second:
+        copy.wait()
+    mean = jnp.where(belongs(0), own_mean, 0.0)
+    for o in range(1, len(offsets)):
+        mean = mean + jnp.where(belongs(o), mean_in[o][:, 0:1], 0.0)
+    mean = jnp.sum(mean, axis=0, keepdims=True)
+    neutral = (charges - mean) * live
+
+    x_charged = x_rows[0, :CX] * neutral
+    for y in range(EXT_Y):
+        plane[y * CX : (y + 1) * CX, :] = y_rows[0, y : y + 1, :] * x_charged
+    y_charged = y_rows[0] * neutral
+    base = EXT_Y * CX
+    for x in range(3):
+        plane[base + x * HALO_ROWS : base + (x + 1) * HALO_ROWS, :] = (
+            x_rows[0, CX + x : CX + x + 1, :] * y_charged
+        )
+    top = base + 3 * HALO_ROWS
+    plane[top:, :] = jnp.zeros((PLANE - top, atoms), jnp.float32)
+    spread = dot(z_rows[...], plane[...], (1, 1))
+    tables[0].wait()
+    field_out[...] = dot(fz[...], spread, (1, 0)).reshape(field_out.shape)
+
+    def exchange(source, target, send, recv):
+        def copy(o):
+            p = lax.rem(me + o, n)
+            return pltpu.make_async_remote_copy(
+                source.at[p], target.at[me], send.at[o], recv.at[o],
+                device_id=coords(p), device_id_type=MESH,
+            )
+
+        @pl.loop(1, n)
+        def _(o):
+            copy(o).start()
+
+        target[me] = source[me]
+
+        @pl.loop(1, n)
+        def _(o):
+            copy(o).wait()
+
+    exchange(field_out, field_in, field_send, field_recv)
+
+    @pl.loop(1, n)
+    def _(o):
+        inf_copy(o).wait()
+
+    own_inf.wait()
+    for table in tables[1:]:
+        table.wait()
+
+    low = dot(field_in[...].reshape(PLANE, PLANE), gather[...], (0, 0))
+    real, imag = low[:, :NZ], low[:, NZ:]
+    cosine, sine = twiddle[0], twiddle[1]
+    turned = jnp.concatenate(
+        [real * cosine + imag * sine, imag * cosine - real * sine], axis=0
+    )
+    spectrum = dot(inner[...], turned, (1, 0))
+    parts = []
+    for k in range(2):
+        both = kernel_in[k * n // 2 : k * n // 2 + rows] + kernel_in[k * n // 2 + rows : (k + 1) * n // 2]
+        parts.append(both.reshape(LANES, LANES))
+    green = jnp.concatenate(parts, axis=1)
+    filtered = spectrum * jnp.concatenate([green, green], axis=0)
+    back = dot(inner_t[...], filtered, (1, 0))
+    real, imag = back[:PLANE], back[PLANE:]
+    turned = jnp.concatenate(
+        [real * cosine - imag * sine, imag * cosine + real * sine], axis=1
+    )
+    back_out[...] = dot(gather[...], turned, (1, 1)).reshape(back_out.shape)
+    exchange(back_out, back_in, back_send, back_recv)
+
+    scale = 1.0 / float(CX * rows * CY * cols * NZ)
+    potential = dot(back_in[...].reshape(PLANE, PLANE), fz[...] * scale, (0, 0))
+    sampled[0] = dot(potential[:top], z_rows[...], (1, 0))
+    sampled[1] = dot(potential[:top], z_slopes[...], (1, 0))
+    width = 256
+    for k in range(atoms // width):
+        cut = slice(k * width, (k + 1) * width)
+        by_y = by_dy = by_yz = 0.0
+        for y in range(EXT_Y):
+            row = slice(y * CX, (y + 1) * CX)
+            weight = y_rows[0, y : y + 1, cut]
+            by_y = by_y + weight * sampled[0, row, cut]
+            by_dy = by_dy + y_rows[1, y : y + 1, cut] * sampled[0, row, cut]
+            by_yz = by_yz + weight * sampled[1, row, cut]
+        by_x = by_dx = by_xz = 0.0
+        for x in range(3):
+            row = slice(base + x * HALO_ROWS, base + (x + 1) * HALO_ROWS)
+            weight = x_rows[0, CX + x : CX + x + 1, cut]
+            by_x = by_x + weight * sampled[0, row, cut]
+            by_dx = by_dx + x_rows[1, CX + x : CX + x + 1, cut] * sampled[0, row, cut]
+            by_xz = by_xz + weight * sampled[1, row, cut]
+        xs, dxs = x_rows[0, :CX, cut], x_rows[1, :CX, cut]
+        ys, dys = y_rows[0, :, cut], y_rows[1, :, cut]
+
+        def down(values):
+            return jnp.sum(values, axis=0, keepdims=True)
+
+        value = down(xs * by_y) + down(ys * by_x)
+        grad_x = down(dxs * by_y) + down(ys * by_dx)
+        grad_y = down(xs * by_dy) + down(dys * by_x)
+        grad_z = down(xs * by_yz) + down(ys * by_xz)
+        part = neutral[:, cut]
+        energy_ref[:, cut] = 0.5 * part * value
+        forces_ref[0:1, cut] = -part * grad_x
+        forces_ref[1:2, cut] = -part * grad_y
+        forces_ref[2:3, cut] = -part * grad_z
+
+
+def fast_body(plan, charges, structure_id, live_count, cell_index, fraction, influence):
+    rows, cols, offsets = plan
+    n = rows * cols
+    atoms = charges.shape[0]
+    per_col = NZ // cols // n
+    high = CY // rows
+    stored = influence.reshape(per_col, n, high, cols, CX, rows)
+    stored = stored.transpose(1, 2, 4, 0, 3, 5).reshape(n, high * CX, per_col * n)
+    empty = jnp.zeros_like(stored)
+    stored = jnp.where(
+        lax.axis_index("col") % 2 == 0,
+        jnp.concatenate([stored, empty], axis=2),
+        jnp.concatenate([empty, stored], axis=2),
+    )
+    tables = make_tables(rows, cols)
+    vmem = pl.BlockSpec(memory_space=pltpu.VMEM)
+    anywhere = pl.BlockSpec(memory_space=pl.ANY)
+    f32 = jnp.float32
+    lines = NZ // n
+    count = len(offsets)
+    sems = pltpu.SemaphoreType.DMA
+    forces, energy = pl.pallas_call(
+        functools.partial(kernel, plan),
+        out_shape=(
+            jax.ShapeDtypeStruct((3, atoms), f32),
+            jax.ShapeDtypeStruct((1, atoms), f32),
+        ),
+        in_specs=[vmem] * 5 + [anywhere] * 6,
+        out_specs=(vmem, vmem),
+        scratch_shapes=[
+            pltpu.VMEM((NZ, NZ), f32),
+            pltpu.VMEM(tables[1].shape[1:], f32),
+            pltpu.VMEM(tables[2].shape, f32),
+            pltpu.VMEM(tables[3].shape, f32),
+            pltpu.VMEM(tables[4].shape, f32),
+            pltpu.VMEM((NZ, atoms), f32),
+            pltpu.VMEM((NZ, atoms), f32),
+            pltpu.VMEM((PLANE, atoms), f32),
+            pltpu.VMEM((2, 16, atoms), f32),
+            pltpu.VMEM((2, HALO_ROWS, atoms), f32),
+            pltpu.VMEM((count, 2 * S_DEV, LANES), f32),
+            pltpu.VMEM((count, 2 * S_DEV, LANES), f32),
+            pltpu.VMEM((S_DEV, LANES), f32),
+            pltpu.VMEM((count, S_DEV, LANES), f32),
+            pltpu.VMEM((n, high * CX, LANES), f32),
+            pltpu.VMEM((n, lines, PLANE), f32),
+            pltpu.VMEM((n, lines, PLANE), f32),
+            pltpu.VMEM((n, lines, PLANE), f32),
+            pltpu.VMEM((n, lines, PLANE), f32),
+            pltpu.VMEM((2, EXT_Y * CX + 3 * HALO_ROWS, atoms), f32),
+            sems((5,)),
+            sems((count,)), sems((count,)), sems((count,)), sems((count,)),
+            sems((n,)), sems((n,)), sems((n,)), sems((n,)), sems((n,)), sems((n,)),
+        ],
+        compiler_params=pltpu.CompilerParams(
+            collective_id=0, has_side_effects=True, vmem_limit_bytes=48 * 1024 * 1024
+        ),
+        name="ewald_step",
+    )(
+        charges[None, :], structure_id[None, :], live_count[None, :], cell_index, fraction, stored,
+        *[jnp.asarray(t) for t in tables],
+    )
+    return forces, energy[0]
+
+
 def solution(mesh):
+    plan = make_plan(mesh.shape["row"], mesh.shape["col"])
     placed = (
         P(("row", "col")),
         P(("row", "col")),
@@ -161,7 +592,7 @@
         P("col", "row", None),
     )
     return jax.shard_map(
-        body,
+        body if plan is None else functools.partial(fast_body, plan),
         mesh=mesh,
         in_specs=placed,
         out_specs=(P(None, ("row", "col")), P(("row", "col"))),

time: 172 us -> 43 us (0.25)
  blocking collectives: 81.4 us -> 0 us
  Pallas kernels: 0 us -> 37.8 us
  other arithmetic: 32.2 us -> 0.13 us
  matrix products: 19.3 us -> 0 us
  local copies, waits for them, and re-layouts: 20.3 us -> 3.17 us
  starting transfers between devices: 9.49 us -> 0 us
  waiting for transfers between devices: 5.39 us -> 0 us
    all_to_all x4 -> x0, blocking collectives: 41.7 us -> none  [the longest x1 11.4 us: body(): lax.all_to_all(jnp.stack([back_x, back_x_imag]), 'row', split_axis=3, con...]
    psum x1 -> x0, blocking collectives: 39.6 us -> none  [body(): totals, counts = lax.psum((charge_sums, live_sums), ('row', 'col'))]
    pallas_call x0 -> x1, Pallas kernels: none -> 37.8 us  [fast_body(): pl.pallas_call(functools.partial(kernel, plan), out_shape=(jax.ShapeDtype...]
    dot_general x20 -> x0, matrix products: 16.8 us -> none  [the longest x1 3.31 us: body(): lax.dot_general(jnp.concatenate([z_rows, z_slope_rows], axis=0), widened,...]
    scatter-add x3 -> x0, other arithmetic: 15.5 us -> none  [the longest x1 7.75 us: body(): live_sums = jax.ops.segment_sum(live, structure_id, num_segments=structures)]
    ppermute x4 -> x0, starting transfers between devices: 9.49 us -> none  [passed_along(): return lax.ppermute(block, axis, route)]
    gather x1 -> x0, local copies, waits for them, and re-layouts: 6.83 us -> none  [body(): neutral = (charges - jnp.take(totals / counts, structure_id)) * live]
    ppermute x4 -> x0, waiting for transfers between devices: 5.39 us -> none  [passed_along(): return lax.ppermute(block, axis, route)]
  transfers between devices with their start and end apart: 4 -> 0, of which waited for: 3 -> 0; matrix products, arithmetic and copies ran while one was open for 3% -> 0% of each run, Pallas kernels for 0% -> 0%
where the time goes in v1:
time: 43 us; the launch traced here: 42.8 us
  Pallas kernels  37.8 us (88%)
  local copies, waits for them, and re-layouts  3.17 us (7%)
  between operations  1.69 us (4%)
    pallas_call x1, Pallas kernels, fast_body(): pl.pallas_call(functools.partial(kernel, plan), out_shape=(jax.ShapeDtype...  37.8 us
    unnamed x21, local copies, waits for them, and re-layouts  2.58 us

profile of v1, /device:TPU:9, one launch (start us, length us, event | category | flops | bytes accessed | tf_op | source)
XLA Modules:
  0.0 42.8 jit_solution(18272901882479102243)
XLA Ops:
  0.6 1.1 %copy.14 = f32[64,8,64]{0,2,1:T(8,128)S(1)} copy(f32[64,8,64]{2,1,0:T(8,128)} %param.16) | data formatting | bytes 262144 | tf_op args[5]
  1.7 0.0 copy-start.3
  1.7 0.0 copy-start.5
  1.8 0.0 copy-start.6
  1.8 0.3 reshape.10
  2.1 0.0 copy-start
  2.1 0.1 copy.15
  2.2 0.0 copy-start.1
  2.2 0.0 copy-start.2
  2.2 0.2 copy.16
  2.4 0.0 copy-start.4
  2.4 0.0 copy-start.8
  2.4 0.1 pad_select_fusion.influence_ref
  2.6 0.0 copy-start.7
  3.5 0.0 copy-done.3
  3.5 0.0 copy-done.5
  3.5 0.0 copy-done.6
  3.5 0.0 copy-done
  3.5 0.1 copy-done.2
  3.7 0.1 copy-done.4
  3.8 0.0 copy-done.8
  3.8 37.8 %ewald_step.1 = (f32[3,1024]{1,0:T(4,128)S(1)}, f32[1,1024]{1,0:T(1,128)S(1)}) custom-call(f32[1,1024]{1,0:T(1,128)S(1)} %bitcast.9, s32[1,1024]{1,0:T(1,128)S(1)} %bitcast.10, s32[1,1]{1,0:T(1,128)} %bitcast.8.live_ref, s32[3,1024]{1,0:T(4,128)S(1)} %copy-done.5, f32[3,1024]{1,0:T(4,128)S(1)} %copy-done.6, f32[32,16,128]{2,1,0:T(8,128)S(1)} %pad_select_fusion.influence_ref, ...), custom_call_target="tpu_custom_call" | custom-call | tf_op jit(solution)/shard_map/ewald_step/pallas_call | solution.py:540
  41.6 0.6 %copy.21 = f32[3,1024]{1,0:T(4,128)} copy(f32[3,1024]{1,0:T(4,128)S(1)} %get-tuple-element.8) | data formatting | bytes 24576
  42.2 0.6 %copy.22 = f32[1024]{0:T(1024)} copy(f32[1024]{0:T(1024)S(1)} %bitcast.11) | data formatting | bytes 8192
  (2 shorter events, 0.0 us)
Async XLA Ops:
  1.7 1.8 %copy-start.3 = (f32[512,256]{1,0:T(8,128)S(1)}, f32[512,256]{1,0:T(8,128)}, u32[]{:S(2)}) copy-start(f32[512,256]{1,0:T(8,128)} %constant.34.clone.inner_t_hbm) | copy-start | bytes 1572868
  1.7 1.8 %copy-start.5 = (s32[3,1024]{1,0:T(4,128)S(1)}, s32[3,1024]{1,0:T(4,128)}, u32[]{:S(2)}) copy-start(s32[3,1024]{1,0:T(4,128)} %cell_ref.1) | copy-start | bytes 36868
  1.8 1.8 %copy-start.6 = (f32[3,1024]{1,0:T(4,128)S(1)}, f32[3,1024]{1,0:T(4,128)}, u32[]{:S(2)}) copy-start(f32[3,1024]{1,0:T(4,128)} %frac_ref.1) | copy-start | bytes 36868
  2.1 1.4 %copy-start = (f32[2,256,512]{2,1,0:T(8,128)S(1)}, f32[2,256,512]{2,1,0:T(8,128)}, u32[]{:S(2)}) copy-start(f32[2,256,512]{2,1,0:T(8,128)} %constant.31.clone.gather_hbm) | copy-start | bytes 3145732
  2.2 1.4 %copy-start.1 = (f32[2,256,256]{2,1,0:T(8,128)S(1)}, f32[2,256,256]{2,1,0:T(8,128)}, u32[]{:S(2)}) copy-start(f32[2,256,256]{2,1,0:T(8,128)} %constant.32.clone.twiddle_hbm) | copy-start | bytes 1572868
  2.2 1.5 %copy-start.2 = (f32[256,512]{1,0:T(8,128)S(1)}, f32[256,512]{1,0:T(8,128)}, u32[]{:S(2)}) copy-start(f32[256,512]{1,0:T(8,128)} %constant.33.clone.inner_hbm) | copy-start | bytes 1572868
  2.4 1.4 %copy-start.4 = (f32[256,256]{1,0:T(8,128)S(1)}, f32[256,256]{1,0:T(8,128)}, u32[]{:S(2)}) copy-start(f32[256,256]{1,0:T(8,128)} %constant.30.clone.fz_hbm) | copy-start | bytes 786436
  2.4 1.4 %copy-start.8 = (s32[1024]{0:T(1024)S(1)}, s32[1024]{0:T(1024)}, u32[]{:S(2)}) copy-start(s32[1024]{0:T(1024)} %param.12) | copy-start | bytes 12292
  2.6 1.2 %copy-start.7 = (f32[1024]{0:T(1024)S(1)}, f32[1024]{0:T(1024)}, u32[]{:S(2)}) copy-start(f32[1024]{0:T(1024)} %param.11) | copy-start | bytes 12292

commit v2 on v1

--- a/solution.py
+++ b/solution.py
@@ -189,7 +189,8 @@
         and (NZ // n) % 8 == 0
         and NZ % (cols * n) == 0
         and (CY * cols) % rows == 0
-        and (CY * cols // rows) % cols == 0
+        and CY == 2 * rows
+        and NZ // cols == 2 * n
         and (NZ // n) * n == PLANE
         and NZ // n // 2 * n == LANES
     ):
@@ -242,21 +243,35 @@
     )
     twiddle = np.stack([np.tile(np.cos(psi), (1, slots)), np.tile(np.sin(psi), (1, slots))])
     high_m, high_k = (v.reshape(-1) for v in np.meshgrid(np.arange(CY), np.arange(CX), indexing="ij"))
+    per_row = CY // rows
+    order = np.arange(CY * CX).reshape(rows, per_row, CX).transpose(1, 0, 2).reshape(-1)
+    high_m, high_k = high_m[order], high_k[order]
     chi = 2 * np.pi * (high_k[:, None] * x[None] % CX / CX + high_m[:, None] * y[None] % CY / CY)
     cosc, sinc = np.cos(chi) * used[None], np.sin(chi) * used[None]
     inner = np.block([[cosc, sinc], [-sinc, cosc]])
     tables = (forward_z, gather, twiddle, inner, inner.T)
-    return tuple(np.ascontiguousarray(t).astype(np.float32) for t in tables)
+    pairs = []
+    for table in tables:
+        table = np.asarray(table, np.float32)
+        high = table.astype(jnp.bfloat16)
+        low = (table - high.astype(np.float32)).astype(jnp.bfloat16)
+        pairs.append(np.stack([high, low], axis=-3))
+    pairs[2] = tables[2].astype(np.float32)
+    return tuple(pairs)
+
+
+def split(values):
+    high = values.astype(jnp.bfloat16)
+    return high, (values - high.astype(jnp.float32)).astype(jnp.bfloat16)
 
 
 def dot(left, right, contract):
-    return lax.dot_general(
-        left,
-        right,
-        ((contract[:1], contract[1:]), ((), ())),
-        precision=highest,
-        preferred_element_type=jnp.float32,
-    )
+    def one(a, b):
+        return lax.dot_general(
+            a, b, ((contract[:1], contract[1:]), ((), ())), preferred_element_type=jnp.float32
+        )
+
+    return one(left[0], right[0]) + (one(left[0], right[1]) + one(left[1], right[0]))
 
 
 def pick(distance, weights):
@@ -285,11 +300,11 @@
     atoms = charges_ref.shape[1]
 
     def coords(p):
-        return (p // cols, lax.rem(p, cols))
+        return (lax.div(p, cols), lax.rem(p, cols))
 
     barrier = pltpu.get_barrier_semaphore()
 
-    @pl.loop(1, n)
+    @pl.loop(1, n, unroll=True)
     def _(o):
         pl.semaphore_signal(
             barrier, inc=1, device_id=coords(lax.rem(me + o, n)), device_id_type=MESH
@@ -343,6 +358,27 @@
     for copy in first:
         copy.start()
 
+    place = c * rows + r
+
+    def inf_copy(o):
+        p = lax.rem(me + o, n)
+        residue = jnp.where(c < cols // 2, p, lax.rem(n - p, n))
+        return pltpu.make_async_remote_copy(
+            influence_ref.at[residue], kernel_in.at[place], inf_send.at[o], inf_recv.at[o],
+            device_id=coords(p), device_id_type=MESH,
+        )
+
+    @pl.loop(1, n, unroll=True)
+    def _(o):
+        inf_copy(o).start()
+
+    own_inf = pltpu.make_async_copy(
+        influence_ref.at[jnp.where(c < cols // 2, me, lax.rem(n - me, n))],
+        kernel_in.at[place],
+        inf_recv.at[0],
+    )
+    own_inf.start()
+
     wx, vx = spline_weights(frac_ref[0:1, :])
     wy, vy = spline_weights(frac_ref[1:2, :])
     wz, vz = spline_weights(frac_ref[2:3, :])
@@ -354,8 +390,9 @@
         start = pl.multiple_of(b * step, step)
         index = lax.broadcasted_iota(jnp.int32, (step, atoms), 0) + start - cell_z
         distance = jnp.where(index < 0, index + NZ, index)
-        z_rows[pl.ds(start, step), :] = pick(distance, wz)
-        z_slopes[pl.ds(start, step), :] = pick(distance, vz)
+        z_rows[0, pl.ds(start, step), :], z_rows[1, pl.ds(start, step), :] = split(
+            pick(distance, wz)
+        )
 
     distance = lax.broadcasted_iota(jnp.int32, (16, atoms), 0) - (cell_ref[0:1, :] - r * CX)
     x_rows[0] = pick(distance, wx)
@@ -385,26 +422,14 @@
     for copy in second:
         copy.start()
 
-    place = c * rows + r
-
-    def inf_copy(o):
-        p = lax.rem(me + o, n)
-        residue = jnp.where(c < cols // 2, p, lax.rem(n - p, n))
-        return pltpu.make_async_remote_copy(
-            influence_ref.at[residue], kernel_in.at[place], inf_send.at[o], inf_recv.at[o],
-            device_id=coords(p), device_id_type=MESH,
-        )
-
-    @pl.loop(1, n)
-    def _(o):
-        inf_copy(o).start()
-
-    own_inf = pltpu.make_async_copy(
-        influence_ref.at[jnp.where(c < cols // 2, me, lax.rem(n - me, n))],
-        kernel_in.at[place],
-        inf_recv.at[0],
-    )
-    own_inf.start()
+    @pl.loop(0, NZ // step)
+    def _(b):
+        start = pl.multiple_of(b * step, step)
+        index = lax.broadcasted_iota(jnp.int32, (step, atoms), 0) + start - cell_z
+        distance = jnp.where(index < 0, index + NZ, index)
+        z_slopes[0, pl.ds(start, step), :], z_slopes[1, pl.ds(start, step), :] = split(
+            pick(distance, vz)
+        )
 
     for copy in second:
         copy.wait()
@@ -425,9 +450,9 @@
         )
     top = base + 3 * HALO_ROWS
     plane[top:, :] = jnp.zeros((PLANE - top, atoms), jnp.float32)
-    spread = dot(z_rows[...], plane[...], (1, 1))
+    spread = dot((z_rows[0], z_rows[1]), split(plane[...]), (1, 1))
     tables[0].wait()
-    field_out[...] = dot(fz[...], spread, (1, 0)).reshape(field_out.shape)
+    field_out[...] = dot((fz[0], fz[1]), split(spread), (1, 0)).reshape(field_out.shape)
 
     def exchange(source, target, send, recv):
         def copy(o):
@@ -437,51 +462,61 @@
                 device_id=coords(p), device_id_type=MESH,
             )
 
-        @pl.loop(1, n)
+        @pl.loop(1, n, unroll=True)
         def _(o):
             copy(o).start()
 
         target[me] = source[me]
 
-        @pl.loop(1, n)
+        @pl.loop(1, n, unroll=True)
         def _(o):
-            copy(o).wait()
+            pltpu.make_async_remote_copy(
+                source.at[0], target.at[0], send.at[o], recv.at[o],
+                device_id=(r, c), device_id_type=MESH,
+            ).wait()
 
     exchange(field_out, field_in, field_send, field_recv)
 
-    @pl.loop(1, n)
+    @pl.loop(1, n, unroll=True)
     def _(o):
-        inf_copy(o).wait()
+        pltpu.make_async_remote_copy(
+            influence_ref.at[0], kernel_in.at[0], inf_send.at[o], inf_recv.at[o],
+            device_id=(r, c), device_id_type=MESH,
+        ).wait()
 
     own_inf.wait()
     for table in tables[1:]:
         table.wait()
 
-    low = dot(field_in[...].reshape(PLANE, PLANE), gather[...], (0, 0))
+    low = dot(split(field_in[...].reshape(PLANE, PLANE).T), (gather[0], gather[1]), (1, 0))
     real, imag = low[:, :NZ], low[:, NZ:]
     cosine, sine = twiddle[0], twiddle[1]
     turned = jnp.concatenate(
         [real * cosine + imag * sine, imag * cosine - real * sine], axis=0
     )
-    spectrum = dot(inner[...], turned, (1, 0))
-    parts = []
-    for k in range(2):
-        both = kernel_in[k * n // 2 : k * n // 2 + rows] + kernel_in[k * n // 2 + rows : (k + 1) * n // 2]
-        parts.append(both.reshape(LANES, LANES))
-    green = jnp.concatenate(parts, axis=1)
+    spectrum = dot((inner[0], inner[1]), split(turned), (1, 0))
+    by_col = kernel_in[...].reshape(cols, rows * CX, LANES)
+    swapped = [pltpu.roll(by_col[k], LANES // 2, 1) for k in range(cols)]
+    first_half = lax.broadcasted_iota(jnp.int32, (rows * CX, LANES), 1) < LANES // 2
+    lower = [jnp.where(first_half, by_col[k], swapped[k + 1]) for k in range(0, cols, 2)]
+    upper = [jnp.where(first_half, swapped[k], by_col[k + 1]) for k in range(0, cols, 2)]
+    green = jnp.concatenate(
+        [jnp.concatenate(lower, axis=1), jnp.concatenate(upper, axis=1)], axis=0
+    )
     filtered = spectrum * jnp.concatenate([green, green], axis=0)
-    back = dot(inner_t[...], filtered, (1, 0))
+    back = dot((inner_t[0], inner_t[1]), split(filtered), (1, 0))
     real, imag = back[:PLANE], back[PLANE:]
     turned = jnp.concatenate(
         [real * cosine - imag * sine, imag * cosine + real * sine], axis=1
     )
-    back_out[...] = dot(gather[...], turned, (1, 1)).reshape(back_out.shape)
+    back_out[...] = dot((gather[0], gather[1]), split(turned), (1, 1)).reshape(back_out.shape)
     exchange(back_out, back_in, back_send, back_recv)
 
     scale = 1.0 / float(CX * rows * CY * cols * NZ)
-    potential = dot(back_in[...].reshape(PLANE, PLANE), fz[...] * scale, (0, 0))
-    sampled[0] = dot(potential[:top], z_rows[...], (1, 0))
-    sampled[1] = dot(potential[:top], z_slopes[...], (1, 0))
+    potential = dot(split(back_in[...].reshape(PLANE, PLANE).T), (fz[0], fz[1]), (1, 0))
+    potential = split(potential[:top] * scale)
+    sampled[0] = dot(potential, (z_rows[0], z_rows[1]), (1, 0))
+    sampled[1] = dot(potential, (z_slopes[0], z_slopes[1]), (1, 0))
     width = 256
     for k in range(atoms // width):
         cut = slice(k * width, (k + 1) * width)
@@ -523,16 +558,10 @@
     per_col = NZ // cols // n
     high = CY // rows
     stored = influence.reshape(per_col, n, high, cols, CX, rows)
-    stored = stored.transpose(1, 2, 4, 0, 3, 5).reshape(n, high * CX, per_col * n)
-    empty = jnp.zeros_like(stored)
-    stored = jnp.where(
-        lax.axis_index("col") % 2 == 0,
-        jnp.concatenate([stored, empty], axis=2),
-        jnp.concatenate([empty, stored], axis=2),
-    )
+    stored = stored.transpose(1, 4, 2, 0, 3, 5).reshape(n, CX, high * per_col * n)
     tables = make_tables(rows, cols)
     vmem = pl.BlockSpec(memory_space=pltpu.VMEM)
-    anywhere = pl.BlockSpec(memory_space=pl.ANY)
+    anywhere = pl.BlockSpec(memory_space=pltpu.HBM)
     f32 = jnp.float32
     lines = NZ // n
     count = len(offsets)
@@ -546,13 +575,13 @@
         in_specs=[vmem] * 5 + [anywhere] * 6,
         out_specs=(vmem, vmem),
         scratch_shapes=[
-            pltpu.VMEM((NZ, NZ), f32),
-            pltpu.VMEM(tables[1].shape[1:], f32),
+            pltpu.VMEM(tables[0].shape, jnp.bfloat16),
+            pltpu.VMEM(tables[1].shape[1:], jnp.bfloat16),
             pltpu.VMEM(tables[2].shape, f32),
-            pltpu.VMEM(tables[3].shape, f32),
-            pltpu.VMEM(tables[4].shape, f32),
-            pltpu.VMEM((NZ, atoms), f32),
-            pltpu.VMEM((NZ, atoms), f32),
+            pltpu.VMEM(tables[3].shape, jnp.bfloat16),
+            pltpu.VMEM(tables[4].shape, jnp.bfloat16),
+            pltpu.VMEM((2, NZ, atoms), jnp.bfloat16),
+            pltpu.VMEM((2, NZ, atoms), jnp.bfloat16),
             pltpu.VMEM((PLANE, atoms), f32),
             pltpu.VMEM((2, 16, atoms), f32),
             pltpu.VMEM((2, HALO_ROWS, atoms), f32),
@@ -560,7 +589,7 @@
             pltpu.VMEM((count, 2 * S_DEV, LANES), f32),
             pltpu.VMEM((S_DEV, LANES), f32),
             pltpu.VMEM((count, S_DEV, LANES), f32),
-            pltpu.VMEM((n, high * CX, LANES), f32),
+            pltpu.VMEM((n, CX, LANES), f32),
             pltpu.VMEM((n, lines, PLANE), f32),
             pltpu.VMEM((n, lines, PLANE), f32),
             pltpu.VMEM((n, lines, PLANE), f32),

time: 43 us -> 40.1 us (0.933)
  Pallas kernels: 37.8 us -> 33.6 us
  local copies, waits for them, and re-layouts: 3.17 us -> 4.85 us
    pallas_call x1, Pallas kernels: 37.8 us -> 33.6 us  [fast_body(): pl.pallas_call(functools.partial(kernel, plan), out_shape=(jax.ShapeDtype...]
    reshape x1, local copies, waits for them, and re-layouts: 0.21 us -> 1.28 us  [fast_body(): stored.transpose(1, 4, 2, 0, 3, 5).reshape(n, CX, high * per_col * n)]
    transpose x1, local copies, waits for them, and re-layouts: 0.06 us -> 0.87 us  [fast_body(): stored.transpose(1, 4, 2, 0, 3, 5).reshape(n, CX, high * per_col * n)]
where the time goes in v2:
time: 40.1 us; the launch traced here: 39.9 us
  Pallas kernels  33.6 us (84%)
  local copies, waits for them, and re-layouts  4.85 us (12%)
  between operations  1.44 us (4%)
    pallas_call x1, Pallas kernels, fast_body(): pl.pallas_call(functools.partial(kernel, plan), out_shape=(jax.ShapeDtype...  33.6 us
    unnamed x21, local copies, waits for them, and re-layouts  2.39 us
    reshape x1, local copies, waits for them, and re-layouts, fast_body(): stored.transpose(1, 4, 2, 0, 3, 5).reshape(n, CX, high * per_col * n)  1.28 us
    transpose x1, local copies, waits for them, and re-layouts, fast_body(): stored.transpose(1, 4, 2, 0, 3, 5).reshape(n, CX, high * per_col * n)  0.87 us

profile of v2, /device:TPU:9, one launch (start us, length us, event | category | flops | bytes accessed | tf_op | source)
XLA Modules:
  0.0 39.9 jit_solution(3168577265088093614)
XLA Ops:
  0.6 0.0 copy-start.3
  0.6 1.1 %copy.14 = f32[64,8,64]{0,2,1:T(8,128)S(1)} copy(f32[64,8,64]{2,1,0:T(8,128)} %param.16) | data formatting | bytes 262144 | tf_op args[5]
  1.8 0.0 copy-start.2
  1.8 0.0 copy-start.4
  1.8 0.3 reshape.10
  2.1 0.0 copy-start
  2.2 0.9 %copy.15 = f32[32,8,2,2,4,8]{0,5,4,3,2,1:T(8,128)} copy(f32[32,8,2,2,4,8]{0,3,5,1,4,2:T(2,128)S(1)} %bitcast.13) | data formatting | bytes 262144 | tf_op jit(solution)/shard_map/transpose | solution.py:561
  3.0 0.0 copy-start.1
  3.0 0.0 copy-start.5
  3.0 0.0 copy-start.6
  3.0 1.3 %copy.16.influence_ref = f32[32,8,128]{2,1,0:T(8,128)S(1)} copy(f32[32,8,128]{0,2,1:T(8,128)} %bitcast.12) | data formatting | bytes 262144 | tf_op jit(solution)/shard_map/reshape | solution.py:561
  4.3 0.0 copy-start.7
  5.0 0.0 copy-done.3
  5.0 0.0 copy-done.2
  5.0 0.0 copy-done.4
  5.0 0.0 copy-done
  5.0 0.0 copy-done.1
  5.0 0.0 copy-done.5
  5.0 0.0 copy-done.6
  5.1 0.0 copy-done.8
  5.1 0.0 copy-done.7
  5.1 33.6 %ewald_step.1 = (f32[3,1024]{1,0:T(4,128)S(1)}, f32[1,1024]{1,0:T(1,128)S(1)}) custom-call(f32[1,1024]{1,0:T(1,128)S(1)} %bitcast.9, s32[1,1024]{1,0:T(1,128)S(1)} %bitcast.10, s32[1,1]{1,0:T(1,128)} %bitcast.8.live_ref, s32[3,1024]{1,0:T(4,128)S(1)} %copy-done.5, f32[3,1024]{1,0:T(4,128)S(1)} %copy-done.6, f32[32,8,128]{2,1,0:T(8,128)S(1)} %copy.16.influence_ref, ...), custom_call_target="tpu_custom_call" | custom-call | tf_op jit(solution)/shard_map/ewald_step/pallas_call | solution.py:569
  38.7 0.6 %copy.20 = f32[3,1024]{1,0:T(4,128)} copy(f32[3,1024]{1,0:T(4,128)S(1)} %get-tuple-element.8) | data formatting | bytes 24576
  39.3 0.6 %copy.21 = f32[1024]{0:T(1024)} copy(f32[1024]{0:T(1024)S(1)} %bitcast.11) | data formatting | bytes 8192
  (1 shorter events, 0.0 us)
Async XLA Ops:
  0.6 4.4 %copy-start.3 = (bf16[2,512,256]{2,1,0:T(8,128)(2,1)S(1)}, bf16[2,512,256]{2,1,0:T(8,128)(2,1)}, u32[]{:S(2)}) copy-start(bf16[2,512,256]{2,1,0:T(8,128)(2,1)} %constant.14.clone.inner_t_hbm) | copy-start | bytes 1572868
  1.8 3.2 %copy-start.2 = (bf16[2,256,512]{2,1,0:T(8,128)(2,1)S(1)}, bf16[2,256,512]{2,1,0:T(8,128)(2,1)}, u32[]{:S(2)}) copy-start(bf16[2,256,512]{2,1,0:T(8,128)(2,1)} %constant.13.clone.inner_hbm) | copy-start | bytes 1572868
  1.8 3.2 %copy-start.4 = (bf16[2,256,256]{2,1,0:T(8,128)(2,1)S(1)}, bf16[2,256,256]{2,1,0:T(8,128)(2,1)}, u32[]{:S(2)}) copy-start(bf16[2,256,256]{2,1,0:T(8,128)(2,1)} %constant.10.clone.fz_hbm) | copy-start | bytes 786436
  2.1 2.9 %copy-start = (bf16[2,2,256,512]{3,2,1,0:T(8,128)(2,1)S(1)}, bf16[2,2,256,512]{3,2,1,0:T(8,128)(2,1)}, u32[]{:S(2)}) copy-start(bf16[2,2,256,512]{3,2,1,0:T(8,128)(2,1)} %constant.11.clone.gather_hbm) | copy-start | bytes 3145732
  3.0 2.0 %copy-start.1 = (f32[2,256,256]{2,1,0:T(8,128)S(1)}, f32[2,256,256]{2,1,0:T(8,128)}, u32[]{:S(2)}) copy-start(f32[2,256,256]{2,1,0:T(8,128)} %constant.12.clone.twiddle_hbm) | copy-start | bytes 1572868
  3.0 2.0 %copy-start.5 = (s32[3,1024]{1,0:T(4,128)S(1)}, s32[3,1024]{1,0:T(4,128)}, u32[]{:S(2)}) copy-start(s32[3,1024]{1,0:T(4,128)} %cell_ref.1) | copy-start | bytes 36868
  3.0 2.0 %copy-start.6 = (f32[3,1024]{1,0:T(4,128)S(1)}, f32[3,1024]{1,0:T(4,128)}, u32[]{:S(2)}) copy-start(f32[3,1024]{1,0:T(4,128)} %frac_ref.1) | copy-start | bytes 36868
  3.0 2.0 %copy-start.8 = (s32[1024]{0:T(1024)S(1)}, s32[1024]{0:T(1024)}, u32[]{:S(2)}) copy-start(s32[1024]{0:T(1024)} %param.12) | copy-start | bytes 12292
  4.3 0.8 %copy-start.7 = (f32[1024]{0:T(1024)S(1)}, f32[1024]{0:T(1024)}, u32[]{:S(2)}) copy-start(f32[1024]{0:T(1024)} %param.11) | copy-start | bytes 12292
